TPU v7x, 256 devices: a whole 4x4x8 slice. The times are simulated.
256 devices in a mesh: member: 8 (over y, z_hi), tile: 32 (over z_lo, x, core).
Axes of the slice: x: 4, y: 4, z: 8 (z_hi: 2, z_lo: 4; z = z_hi * 4 + z_lo), core: 2. Of those that a mesh axis runs over, the one named last changes fastest.
Arguments:
- surface: float32 [16, 1024, 512], P('member', 'tile'), may hold values from -6 to 6
- depth: float32 [1024, 512], P('tile'), may hold values from 0.32 to 0.45
- land: int32 [1024, 512], P('tile'), may hold values from 0 to 1, as said below
- gauge_cells: int32 [400], replicated, may hold values from 0 to 524287, as said below
- sigma: float32 [400], replicated, may hold values from 0.2 to 1
- observed: float32 [9600], replicated, may hold values from -4 to 4
- noise: float32 [16, 9600], P('member'), may hold values from -3 to 3
Outputs:
- updated: float32 [16, 1024, 512], P('member', 'tile')
- records: float32 [16, 9600], P('member', 'tile')
Inputs may be any that keep to these rules, and one draw needn't show every extreme that they name: `gauge_cells`: every block of 32 rows starting at a multiple of 32 holds a gauge in its first row and one in its last row. `land`: every gauge cell and the cells directly above and below it (rows taken periodically) are sea.
All inputs are finite; a program needn't handle non-finite values.
Results may differ from a plain program's by a relative error of at most 0.00022.
Values sent between devices are 32-bit elements; how exact they have to be, the bound alone decides.
A program may use at most 64 MiB of HBM per device.

v0:
```python
import jax
import jax.numpy as jnp
from jax import lax
from jax.sharding import PartitionSpec as P

STEPS = 24


def shifted(value, axis, steps):
    count = lax.axis_size(axis)
    pairs = [(source, (source + steps) % count) for source in range(count)]
    return lax.ppermute(value, axis, pairs)


def chol_solve(factor, rhs):
    middle = lax.linalg.triangular_solve(factor, rhs, left_side=True, lower=True, transpose_a=False)
    return lax.linalg.triangular_solve(factor, middle, left_side=True, lower=True, transpose_a=True)


def member_grams(gathered, weight):
    all_records, all_innovation = gathered
    anomaly = all_records - jnp.mean(all_records, axis=0, keepdims=True)
    weighted = anomaly * weight[None, :]
    gram_ss = jnp.dot(weighted, anomaly.T, precision=lax.Precision.HIGHEST)
    gram_se = jnp.dot(weighted, all_innovation.T, precision=lax.Precision.HIGHEST)
    return (gram_ss, gram_se)


def shards(surface, depth, land, gauge_cells, sigma, observed, noise):
    member_dev, row_count, col_count = surface.shape
    tile_count = lax.axis_size("tile")
    member_total = member_dev * lax.axis_size("member")
    wet_depth = depth * land.astype(jnp.float32)
    cell_count = row_count * col_count
    local_cell = gauge_cells - lax.axis_index("tile") * cell_count
    gauge_here = ((local_cell >= 0) & (local_cell < cell_count)).astype(jnp.float32)
    gauge_pos = jnp.clip(local_cell, 0, cell_count - 1)
    next_first = shifted(wet_depth[0:1], "tile", -1)
    zero_col = jnp.zeros((row_count, 1), jnp.float32)
    coeff_rows = jnp.minimum(wet_depth, jnp.concatenate([wet_depth[1:], next_first], 0))
    coeff_cols = jnp.minimum(wet_depth, jnp.concatenate([wet_depth[:, 1:], zero_col], 1))

    def advance(carry, ignored):
        level, flux_rows, flux_cols = carry
        next_row = shifted(level[:, 0:1, :], "tile", -1)
        member_rows = level.shape[0]
        below = jnp.concatenate([level[:, 1:], next_row], 1)
        flux_rows = flux_rows - coeff_rows * (below - level)
        level_col = jnp.zeros((member_rows, row_count, 1), jnp.float32)
        beside = jnp.concatenate([level[:, :, 1:], level_col], 2)
        flux_cols = flux_cols - coeff_cols * (beside - level)
        prior_row = shifted(flux_rows[:, -1:, :], "tile", 1)
        above = jnp.concatenate([prior_row, flux_rows[:, :-1]], 1)
        left = jnp.concatenate([level_col, flux_cols[:, :, :-1]], 2)
        level = level - (flux_rows - above + flux_cols - left)
        sample = jnp.take(level.reshape(member_dev, -1), gauge_pos, axis=1) * gauge_here[None, :]
        return ((level, flux_rows, flux_cols), sample)

    start = (surface, jnp.zeros_like(surface), jnp.zeros_like(surface))
    final, samples = lax.scan(advance, start, None, length=STEPS)
    partial_records = jnp.transpose(samples, (1, 0, 2)).reshape(member_dev, -1)
    data_count = partial_records.shape[1]
    piece_count = data_count // tile_count
    piece_start = lax.axis_index("tile") * piece_count
    weight = jnp.tile(1.0 / (sigma * sigma), data_count // sigma.shape[0])
    summed = lax.psum(partial_records, "tile")
    innovation = observed[None, :] + noise - summed
    gathered = (
        lax.all_gather(summed, "member", axis=0, tiled=True),
        lax.all_gather(innovation, "member", axis=0, tiled=True),
    )
    gram_ss, gram_se = member_grams(gathered, weight)
    out_records = lax.dynamic_slice_in_dim(summed, piece_start, piece_count, 1)
    identity = jnp.eye(member_total, dtype=jnp.float32)
    system = gram_ss + (member_total - 1.0) * identity
    factor = jnp.linalg.cholesky(system)
    mixing = chol_solve(factor, gram_se)
    combine = identity + mixing - jnp.mean(mixing, axis=0, keepdims=True)
    first_member = lax.axis_index("member") * member_dev
    local_combine = lax.dynamic_slice_in_dim(combine, first_member, member_dev, 1)
    updated = jnp.einsum(
        "kxy,km->mxy",
        lax.all_gather(surface, "member", axis=0, tiled=True),
        local_combine,
        precision=lax.Precision.HIGHEST,
    )
    return (updated, out_records)


def solution(mesh):
    in_specs = (
        P("member", "tile", None),
        P("tile", None),
        P("tile", None),
        P(),
        P(),
        P(),
        P("member", None),
    )
    out_specs = (P("member", "tile", None), P("member", "tile"))
    return jax.shard_map(shards, mesh=mesh, in_specs=in_specs, out_specs=out_specs, check_vma=False)
```

profile of v0, /device:TPU:128, one launch (start us, length us, event | category | flops | bytes accessed | tf_op | source)
XLA Modules:
  0.0 844.5 jit_solution(1827644809511835850)
XLA Ops:
  15.0 451.3 %while.17 = (s32[]{:T(128)}, f32[2,32,512]{2,1,0:T(8,128)S(1)}, f32[2,32,512]{2,1,0:T(8,128)S(1)}, f32[2,32,512]{2,1,0:T(8,128)S(1)}, f32[24,2,400]{1,2,0:T(8,12...) while((s32[]{:T(128)}, f32[2,32,512]{2,1,0:T(8,128)S(1)}, ...), condition=%wide.region_1.2_spmd.clone, body=%wide.region_0.1_spmd.clone.sunk | while | flops 464979 | bytes 2890483 | solution.py:60
  15.0 4.6 collective-permute-start
  21.2 6.9 collective-permute-done.1
  28.2 4.6 copy.37
  32.8 4.5 gather_fusion
  39.8 6.9 collective-permute-done.1
  46.8 4.6 copy.37
  51.4 4.5 gather_fusion
  58.4 6.9 collective-permute-done.1
  65.4 4.6 copy.37
  70.1 4.5 gather_fusion
  77.0 6.9 collective-permute-done.1
  84.1 4.6 copy.37
  88.7 4.5 gather_fusion
  95.6 6.9 collective-permute-done.1
  102.7 4.6 copy.37
  107.3 4.5 gather_fusion
  114.2 6.9 collective-permute-done.1
  121.3 4.6 copy.37
  125.9 4.5 gather_fusion
  132.9 6.9 collective-permute-done.1
  139.9 4.6 copy.37
  144.5 4.5 gather_fusion
  151.5 6.9 collective-permute-done.1
  158.5 4.6 copy.37
  163.1 4.5 gather_fusion
  170.1 6.9 collective-permute-done.1
  177.1 4.6 copy.37
  181.7 4.5 gather_fusion
  188.7 6.9 collective-permute-done.1
  195.7 4.6 copy.37
  207.3 6.9 collective-permute-done.1
  214.3 4.6 copy.37
  225.9 6.9 collective-permute-done.1
  233.0 4.6 copy.37
  244.5 6.9 collective-permute-done.1
  251.6 4.6 copy.37
  263.1 6.9 collective-permute-done.1
  270.2 4.6 copy.37
  274.8 4.5 gather_fusion
  281.7 6.9 collective-permute-done.1
  288.8 4.6 copy.37
  300.3 6.9 collective-permute-done.1
  307.4 4.6 copy.37
  318.9 6.9 collective-permute-done.1
  326.0 4.6 copy.37
  337.6 6.9 collective-permute-done.1
  344.6 4.6 copy.37
  356.2 6.9 collective-permute-done.1
  363.2 4.6 copy.37
  374.8 6.9 collective-permute-done.1
  381.8 4.6 copy.37
  393.4 6.9 collective-permute-done.1
  400.4 4.6 copy.37
  412.0 6.9 collective-permute-done.1
  419.0 4.6 copy.37
  423.7 4.5 gather_fusion
  430.6 6.9 collective-permute-done.1
  437.6 4.6 copy.37
  449.2 6.9 collective-permute-done.1
  456.3 4.6 copy.37
  470.9 256.3 %all-reduce.5.cloned.1.call-done = f32[2,9600]{1,0:T(2,128)} async-done(((f32[2,9600]{1,0:T(2,128)}), f32[2,9600]{1,0:T(2,128)}) %all-reduce.5.cloned.1.call-update) | async-done | bytes 76816 | tf_op jit(solution)/shard_map/psum | solution.py:66
  727.2 48.0 %all-gather = f32[8,2,9600]{2,1,0:T(2,128)S(1)} all-gather(f32[1,2,9600]{2,1,0:T(2,128)} %bitcast.56), channel_id=1, replica_groups=mesh['member'=8,'tile'=32] {'member'}, dimensions={0}, use_global_device_ids=true | all-gather | bytes 691200 | tf_op jit(solution)/shard_map/all_gather | solution.py:69
  781.8 48.7 %all-gather.1 = f32[8,2,9600]{2,1,0:T(2,128)S(1)} all-gather(f32[1,2,9600]{2,1,0:T(2,128)S(1)} %subtract_bitcast_fusion), channel_id=1, replica_groups=mesh['member'=8,'tile'=32] {'member'}, dimensions={0}, use_global_device_ids=true | all-gather | bytes 691200 | tf_op jit(solution)/shard_map/all_gather | solution.py:70
  (376 shorter events, 143.1 us)
Async XLA Ops:
  8.0 719.2 %all-reduce.5.cloned.1.call-start = ((), (), s32[]{:S(2)}) async-start(), calls=%async_computation | async-start | bytes 153600 | tf_op jit(solution)/shard_map/psum | solution.py:66
  8.9 6.0 collective-permute-start.2
  15.0 5.9 collective-permute-start
  21.1 7.0 collective-permute-start.1
  38.2 1.3 collective-permute-start
  39.7 7.0 collective-permute-start.1
  56.8 1.3 collective-permute-start
  58.3 7.0 collective-permute-start.1
  75.5 1.3 collective-permute-start
  76.9 7.0 collective-permute-start.1
  94.1 1.3 collective-permute-start
  95.5 7.0 collective-permute-start.1
  112.7 1.3 collective-permute-start
  114.1 7.0 collective-permute-start.1
  131.3 1.3 collective-permute-start
  132.8 7.0 collective-permute-start.1
  149.9 1.3 collective-permute-start
  151.4 7.0 collective-permute-start.1
  168.5 1.3 collective-permute-start
  170.0 7.0 collective-permute-start.1
  187.1 1.3 collective-permute-start
  188.6 7.0 collective-permute-start.1
  205.7 1.3 collective-permute-start
  207.2 7.0 collective-permute-start.1
  224.4 1.3 collective-permute-start
  225.8 7.0 collective-permute-start.1
  243.0 1.3 collective-permute-start
  244.4 7.0 collective-permute-start.1
  261.6 1.3 collective-permute-start
  263.0 7.0 collective-permute-start.1
  280.2 1.3 collective-permute-start
  281.6 7.0 collective-permute-start.1
  298.8 1.3 collective-permute-start
  300.2 7.0 collective-permute-start.1
  317.4 1.3 collective-permute-start
  318.8 7.0 collective-permute-start.1
  336.0 1.3 collective-permute-start
  337.5 7.0 collective-permute-start.1
  354.6 1.3 collective-permute-start
  356.1 7.0 collective-permute-start.1
  373.2 1.3 collective-permute-start
  374.7 7.0 collective-permute-start.1
  391.8 1.3 collective-permute-start
  393.3 7.0 collective-permute-start.1
  410.4 1.3 collective-permute-start
  411.9 7.0 collective-permute-start.1
  429.0 1.3 collective-permute-start
  430.5 7.0 collective-permute-start.1
  447.7 1.3 collective-permute-start
  449.1 7.0 collective-permute-start.1
  466.3 4.4 copy-start.2
  466.3 312.0 %copy-start = (f32[2,9600]{1,0:T(2,128)S(1)}, f32[2,9600]{1,0:T(2,128)}, u32[]{:S(2)}) copy-start(f32[2,9600]{1,0:T(2,128)} %param.15) | copy-start | bytes 230404
  466.3 312.0 %copy-start.1 = (f32[9600]{0:T(1024)S(1)}, f32[9600]{0:T(1024)}, u32[]{:S(2)}) copy-start(f32[9600]{0:T(1024)} %param.14) | copy-start | bytes 115204
  470.1 363.8 %all-gather.4.cloned.1.call-start = ((), (), s32[]{:S(2)}) async-start(), calls=%async_computation.1 | async-start | bytes 1179648 | tf_op jit(solution)/shard_map/all_gather | solution.py:83
Sparse Core Ops, SparseCore 0:
  470.2 256.9 all-reduce.4
Sparse Core Ops, SparseCore 1:
  473.2 51.3 all-gather.3
where the time goes:
time: 846 us; the launch traced here: 844 us
  waiting for transfers between devices  451 us (53%)
  local copies, waits for them, and re-layouts  230 us (27%)
  blocking collectives  96.7 us (11%)
  other arithmetic  34.2 us (4%)
  between operations  15.6 us (2%)
  starting transfers between devices  10.4 us (1%)
    psum x1, waiting for transfers between devices, shards(): summed = lax.psum(partial_records, 'tile')  256 us
    ppermute x49, waiting for transfers between devices, shifted(): return lax.ppermute(value, axis, pairs)  194 us
    sub x24, local copies, waits for them, and re-layouts, advance(): level = level - (flux_rows - above + flux_cols - left)  111 us
    gather x24, local copies, waits for them, and re-layouts, advance(): jnp.take(level.reshape(member_dev, -1), gauge_pos, axis=1)  108 us
    all_gather x1, blocking collectives, shards(): lax.all_gather(innovation, 'member', axis=0, tiled=True)  48.7 us
    all_gather x1, blocking collectives, shards(): lax.all_gather(summed, 'member', axis=0, tiled=True)  48 us
    dynamic_update_slice x24, other arithmetic, shards(): final, samples = lax.scan(advance, start, None, length=STEPS)  20.8 us
  transfers between devices with their start and end apart: 51, of which 49 were waited for; matrix products, arithmetic and copies ran while one was open for 2% of the time, Pallas kernels for 0%

commit v1 on v0

--- a/solution.py
+++ b/solution.py
@@ -67,7 +67,10 @@
     innovation = observed[None, :] + noise - summed
     gathered = (
         lax.all_gather(summed, "member", axis=0, tiled=True),
-        lax.all_gather(innovation, "member", axis=0, tiled=True),
+        jnp.concatenate(
+            lax.all_to_all(jnp.stack([innovation] * lax.axis_size("member")), "member", 0, 0),
+            axis=0,
+        ),
     )
     gram_ss, gram_se = member_grams(gathered, weight)
     out_records = lax.dynamic_slice_in_dim(summed, piece_start, piece_count, 1)

time: 846 us -> 819 us (0.968)
  blocking collectives: 96.7 us -> 53.7 us
  starting transfers between devices: 10.4 us -> 19.9 us
    all_gather x1 -> x0, blocking collectives: 48.7 us -> none  [shards(): lax.all_gather(innovation, 'member', axis=0, tiled=True)]
    all_to_all x0 -> x1, starting transfers between devices: none -> 9.51 us  [shards(): lax.all_to_all(jnp.stack([innovation] * lax.axis_size('member')), 'member...]
  transfers between devices with their start and end apart: 51 -> 52, of which waited for: 49 -> 50; matrix products, arithmetic and copies ran while one was open for 2% -> 2% of each run, Pallas kernels for 0% -> 0%
where the time goes in v1:
time: 819 us; the launch traced here: 813 us
  waiting for transfers between devices  452 us (55%)
  local copies, waits for them, and re-layouts  231 us (28%)
  blocking collectives  53.7 us (7%)
  other arithmetic  34.2 us (4%)
  starting transfers between devices  19.9 us (2%)
  between operations  15.6 us (2%)
    psum x1, waiting for transfers between devices, shards(): summed = lax.psum(partial_records, 'tile')  256 us
    ppermute x49, waiting for transfers between devices, shifted(): return lax.ppermute(value, axis, pairs)  194 us
    sub x24, local copies, waits for them, and re-layouts, advance(): level = level - (flux_rows - above + flux_cols - left)  111 us
    gather x24, local copies, waits for them, and re-layouts, advance(): jnp.take(level.reshape(member_dev, -1), gauge_pos, axis=1)  108 us
    all_gather x1, blocking collectives, shards(): lax.all_gather(summed, 'member', axis=0, tiled=True)  53.7 us
    dynamic_update_slice x24, other arithmetic, shards(): final, samples = lax.scan(advance, start, None, length=STEPS)  20.8 us
  transfers between devices with their start and end apart: 52, of which 50 were waited for; matrix products, arithmetic and copies ran while one was open for 2% of the time, Pallas kernels for 0%

profile of v1, /device:TPU:128, one launch (start us, length us, event | category | flops | bytes accessed | tf_op | source)
XLA Modules:
  0.0 812.8 jit_solution(15311462430397097585)
XLA Ops:
  15.0 451.2 %while.17 = (s32[]{:T(128)}, f32[2,32,512]{2,1,0:T(8,128)S(1)}, f32[2,32,512]{2,1,0:T(8,128)S(1)}, f32[2,32,512]{2,1,0:T(8,128)S(1)}, f32[24,2,400]{1,2,0:T(8,12...) while((s32[]{:T(128)}, f32[2,32,512]{2,1,0:T(8,128)S(1)}, ...), condition=%wide.region_1.2_spmd.clone, body=%wide.region_0.1_spmd.clone.sunk | while | flops 464979 | bytes 2890483 | solution.py:60
  15.0 4.6 collective-permute-start
  21.2 6.9 collective-permute-done.1
  28.2 4.6 copy.37
  32.8 4.5 gather_fusion
  39.8 6.9 collective-permute-done.1
  46.8 4.6 copy.37
  51.4 4.5 gather_fusion
  58.4 6.9 collective-permute-done.1
  65.4 4.6 copy.37
  70.1 4.5 gather_fusion
  77.0 6.9 collective-permute-done.1
  84.1 4.6 copy.37
  88.7 4.5 gather_fusion
  95.6 6.9 collective-permute-done.1
  102.7 4.6 copy.37
  107.3 4.5 gather_fusion
  114.3 6.9 collective-permute-done.1
  121.3 4.6 copy.37
  125.9 4.5 gather_fusion
  132.9 6.9 collective-permute-done.1
  139.9 4.6 copy.37
  144.5 4.5 gather_fusion
  151.5 6.9 collective-permute-done.1
  158.5 4.6 copy.37
  163.1 4.5 gather_fusion
  170.1 6.9 collective-permute-done.1
  177.1 4.6 copy.37
  181.7 4.5 gather_fusion
  188.7 6.9 collective-permute-done.1
  195.7 4.6 copy.37
  200.3 4.5 gather_fusion
  207.3 6.9 collective-permute-done.1
  214.3 4.6 copy.37
  218.9 4.5 gather_fusion
  225.9 6.9 collective-permute-done.1
  232.9 4.6 copy.37
  244.5 6.9 collective-permute-done.1
  251.5 4.6 copy.37
  263.1 6.9 collective-permute-done.1
  270.1 4.6 copy.37
  281.7 6.9 collective-permute-done.1
  288.7 4.6 copy.37
  300.3 6.9 collective-permute-done.1
  307.3 4.6 copy.37
  318.9 6.9 collective-permute-done.1
  325.9 4.6 copy.37
  337.5 6.9 collective-permute-done.1
  344.5 4.6 copy.37
  356.1 6.9 collective-permute-done.1
  363.1 4.6 copy.37
  374.7 6.9 collective-permute-done.1
  381.7 4.6 copy.37
  393.3 6.9 collective-permute-done.1
  400.3 4.6 copy.37
  411.9 6.9 collective-permute-done.1
  419.0 4.6 copy.37
  430.5 6.9 collective-permute-done.1
  437.6 4.6 copy.37
  449.1 6.9 collective-permute-done.1
  456.2 4.6 copy.37
  470.8 256.3 %all-reduce.5.cloned.1.call-done = f32[2,9600]{1,0:T(2,128)} async-done(((f32[2,9600]{1,0:T(2,128)}), f32[2,9600]{1,0:T(2,128)}) %all-reduce.5.cloned.1.call-update) | async-done | bytes 76816 | tf_op jit(solution)/shard_map/psum | solution.py:66
  727.1 53.7 %all-gather = f32[8,2,9600]{2,1,0:T(2,128)S(1)} all-gather(f32[1,2,9600]{2,1,0:T(2,128)} %bitcast.54), channel_id=1, replica_groups=mesh['member'=8,'tile'=32] {'member'}, dimensions={0}, use_global_device_ids=true | all-gather | bytes 691200 | tf_op jit(solution)/shard_map/all_gather | solution.py:69
  782.7 9.5 %all-to-all-start = ((f32[8,2,9600]{2,1,0:T(2,128)}), f32[8,2,9600]{2,1,0:T(2,128)S(1)}, u32[]{:S(2)}, u32[]{:S(2)}) async-start(f32[8,2,9600]{2,1,0:T(2,128)} %stack.2), calls=%async_computation | async-start | bytes 1228800 | tf_op jit(solution)/shard_map/all_to_all | solution.py:71
  (378 shorter events, 145.0 us)
Async XLA Ops:
  8.0 719.1 %all-reduce.5.cloned.1.call-start = ((), (), s32[]{:S(2)}) async-start(), calls=%async_computation.1 | async-start | bytes 153600 | tf_op jit(solution)/shard_map/psum | solution.py:66
  8.9 6.0 collective-permute-start.2
  15.0 5.9 collective-permute-start
  21.1 7.0 collective-permute-start.1
  38.2 1.3 collective-permute-start
  39.7 7.0 collective-permute-start.1
  56.8 1.3 collective-permute-start
  58.3 7.0 collective-permute-start.1
  75.5 1.3 collective-permute-start
  76.9 7.0 collective-permute-start.1
  94.1 1.3 collective-permute-start
  95.5 7.0 collective-permute-start.1
  112.7 1.3 collective-permute-start
  114.1 7.0 collective-permute-start.1
  131.3 1.3 collective-permute-start
  132.7 7.0 collective-permute-start.1
  149.9 1.3 collective-permute-start
  151.4 7.0 collective-permute-start.1
  168.5 1.3 collective-permute-start
  170.0 7.0 collective-permute-start.1
  187.1 1.3 collective-permute-start
  188.5 7.0 collective-permute-start.1
  205.7 1.3 collective-permute-start
  207.2 7.0 collective-permute-start.1
  224.3 1.3 collective-permute-start
  225.8 7.0 collective-permute-start.1
  242.9 1.3 collective-permute-start
  244.4 7.0 collective-permute-start.1
  261.5 1.3 collective-permute-start
  263.0 7.0 collective-permute-start.1
  280.1 1.3 collective-permute-start
  281.6 7.0 collective-permute-start.1
  298.7 1.3 collective-permute-start
  300.2 7.0 collective-permute-start.1
  317.3 1.3 collective-permute-start
  318.8 7.0 collective-permute-start.1
  335.9 1.3 collective-permute-start
  337.4 7.0 collective-permute-start.1
  354.5 1.3 collective-permute-start
  356.0 7.0 collective-permute-start.1
  373.1 1.3 collective-permute-start
  374.6 7.0 collective-permute-start.1
  391.7 1.3 collective-permute-start
  393.2 7.0 collective-permute-start.1
  410.3 1.3 collective-permute-start
  411.8 7.0 collective-permute-start.1
  429.0 1.3 collective-permute-start
  430.4 7.0 collective-permute-start.1
  447.6 1.3 collective-permute-start
  449.0 7.0 collective-permute-start.1
  466.2 4.4 copy-start.2
  466.2 314.6 %copy-start = (f32[2,9600]{1,0:T(2,128)S(1)}, f32[2,9600]{1,0:T(2,128)}, u32[]{:S(2)}) copy-start(f32[2,9600]{1,0:T(2,128)} %param.15) | copy-start | bytes 230404
  466.2 314.6 %copy-start.1 = (f32[9600]{0:T(1024)S(1)}, f32[9600]{0:T(1024)}, u32[]{:S(2)}) copy-start(f32[9600]{0:T(1024)} %param.14) | copy-start | bytes 115204
  470.0 332.2 %all-gather.3.cloned.1.call-start = ((), (), s32[]{:S(2)}) async-start(), calls=%async_computation.2 | async-start | bytes 1179648 | tf_op jit(solution)/shard_map/all_gather | solution.py:86
  782.7 17.5 %all-to-all-start = ((f32[8,2,9600]{2,1,0:T(2,128)}), f32[8,2,9600]{2,1,0:T(2,128)S(1)}, u32[]{:S(2)}, u32[]{:S(2)}) async-start(f32[8,2,9600]{2,1,0:T(2,128)} %stack.2), calls=%async_computation | async-start | bytes 1228800 | tf_op jit(solution)/shard_map/all_to_all | solution.py:71
Sparse Core Ops, SparseCore 0:
  470.2 256.9 all-reduce.4
Sparse Core Ops, SparseCore 1:
  473.1 51.3 all-gather.2
